TPU v7x, 32 devices: a whole 2x2x4 slice. The times are simulated.
32 devices in a mesh: tok: 4 (over y, core), ch: 8 (over z, x).
Axes of the slice: x: 2, y: 2, z: 4, core: 2. Of those that a mesh axis runs over, the one named last changes fastest.
Arguments:
- tokens: bfloat16 [4096, 4096], P('tok', 'ch'), may hold values from -6 to 6
- w_in: bfloat16 [4096, 16384], P('tok', 'ch'), may hold values from -0.09375 to 0.09375
- b_in: float32 [16384], P('ch'), may hold values from -3 to 3
- dw_kernel: float32 [9, 16384], P(None, 'ch'), may hold values from -2 to 2
- dw_bias: float32 [16384], P('ch'), may hold values from -3 to 3
- w_out: bfloat16 [16384, 4096], P('ch', 'tok'), may hold values from -0.0625 to 0.0625
- b_out: float32 [4096], P('ch'), may hold values from -3 to 3
Outputs:
- mixed: bfloat16 [4096, 4096], P('tok', 'ch')
All inputs are finite; a program needn't handle non-finite values.
Results may differ from a plain program's by a relative error of at most 0.0055.
Values may be sent and summed in bfloat16 or wider, within the bound.
No kernel may reach another device: no remote copies, remote signals or barrier semaphores. Data moves between devices by JAX's collectives and lax.ppermute only.
A program may use at most 128 MiB of HBM per device.

v0:
```python
import jax
import jax.numpy as jnp
from jax import lax
from jax.sharding import PartitionSpec as P

IMAGES = 2
GRIDW = 64


def with_halo(array, sides, width):
    for axis, dim in sides:
        size, length = (lax.axis_size(axis), array.shape[dim])
        up = [(i, (i + 1) % size) for i in range(size - 1)]
        down = [(j, i) for i, j in up]
        last = lax.slice_in_dim(array, length - width, length, axis=dim)
        initial = lax.slice_in_dim(array, 0, width, axis=dim)
        before = lax.ppermute(last, axis, up)
        after = lax.ppermute(initial, axis, down)
        array = jnp.concatenate([before, array, after], axis=dim)
    return array


def fetch_rims(grid):
    return with_halo(grid, (("tok", 0),), 1)


def conv_taps(padded, taps, bias, height, width):
    conv = bias + jnp.zeros(
        (height,) + padded.shape[1:2] + (width,) + padded.shape[3:], jnp.float32
    )
    for row_off in range(3):
        for col_off in range(3):
            conv = (
                conv
                + taps[3 * row_off + col_off]
                * padded[row_off : row_off + height, :, col_off : col_off + width, :]
            )
    return conv


def pad_columns(grid):
    return jnp.pad(grid, ((0, 0), (0, 0), (1, 1), (0, 0)))


def local(tokens, w_in, b_in, dw_kernel, dw_bias, w_out, b_out):
    rows = tokens.shape[0]
    hidden = w_in.shape[1]
    w_whole = lax.all_gather(w_in, "tok", axis=0, tiled=True)
    summed = jnp.dot(
        lax.all_gather(tokens, "ch", axis=1, tiled=True),
        w_whole,
        preferred_element_type=jnp.float32,
    )
    pre = (summed + b_in).astype(jnp.bfloat16)
    height = rows // (IMAGES * GRIDW)
    grid = pre.reshape(height, IMAGES, GRIDW, hidden)
    padded = pad_columns(fetch_rims(grid).astype(jnp.float32))
    conv = conv_taps(padded, dw_kernel, dw_bias, height, GRIDW)
    act = jax.nn.gelu(conv, approximate=False).astype(jnp.bfloat16).reshape(rows, hidden)
    w_cols = lax.all_gather(w_out, "tok", axis=1, tiled=True)
    flipped = lax.psum_scatter(
        lax.dot_general(w_cols, act, (((0,), (1,)), ((), ())), preferred_element_type=jnp.float32),
        "ch",
        scatter_dimension=0,
        tiled=True,
    )
    return (flipped.T + b_out).astype(jnp.bfloat16)


def solution(mesh):
    in_specs = (
        P("tok", "ch"),
        P("tok", "ch"),
        P("ch"),
        P(None, "ch"),
        P("ch"),
        P("ch", "tok"),
        P("ch"),
    )
    out_specs = P("tok", "ch")
    return jax.shard_map(local, mesh=mesh, in_specs=in_specs, out_specs=out_specs, check_vma=False)
```

profile of v0, /device:TPU:0, one launch (start us, length us, event | category | flops | bytes accessed | tf_op | source)
XLA Modules:
  0.0 669.0 jit_solution(11230460719229125539)
XLA Ops:
  6.5 0.0 copy-start.3
  6.5 0.0 all-gather.4.cloned.1.call-start
  6.5 0.7 all-gather.4.cloned.1.call-update
  7.3 0.0 all-gather.6.cloned.1.call-start
  7.3 0.7 all-gather.6.cloned.1.call-update
  8.0 0.0 all-gather.8.cloned.1.call-start
  8.1 0.7 all-gather.8.cloned.1.call-update
  8.7 0.0 copy-start
  8.8 0.0 reduce-scatter.2.cloned.1.call-start
  8.8 128.3 %all-gather.4.cloned.1.call-done = bf16[1024,4096]{1,0:T(8,128)(2,1)} async-done(((bf16[1024,512]{1,0:T(8,128)(2,1)}), bf16[1024,4096]{1,0:T(8,128)(2,1)}) %all-gather.4.cloned.1.call-update) | async-done | bytes 8388624 | tf_op jit(solution)/shard_map/all_gather | solution.py:50
  137.1 105.7 %all-gather.6.cloned.1.call-done = bf16[4096,2048]{1,0:T(8,128)(2,1)} async-done(((bf16[1024,2048]{1,0:T(8,128)(2,1)}), bf16[4096,2048]{1,0:T(8,128)(2,1)}) %all-gather.6.cloned.1.call-update) | async-done | bytes 16777232 | tf_op jit(solution)/shard_map/all_gather | solution.py:48
  242.7 0.0 copy-done.3
  242.7 22.7 %add_convert_fusion = bf16[1024,2048]{1,0:T(8,128)(2,1)S(1)} fusion(bf16[1024,4096]{1,0:T(8,128)(2,1)} %all-gather.4.cloned.1.call-done, bf16[4096,2048]{1,0:T(8,128)(2,1)} %all-gather.6.cloned.1.call-done, f32[2048]{0:T(1024)S(1)} %copy-done.3), kind=kOutput, calls=%fused_computation.42 | convolution fusion | flops 17184063488 | bytes 29368320 | tf_op jit(solution)/shard_map/dot_general | solution.py:49
  265.4 0.1 fusion.26
  265.6 0.0 copy-start.1
  265.6 1.3 collective-permute-start.1
  266.9 3.1 collective-permute-start
  269.9 0.0 copy-done
  269.9 0.1 fusion.27
  270.0 0.0 collective-permute-done.1
  270.0 1.9 collective-permute-done
  271.9 0.8 maximum_convert_fusion
  272.7 0.0 copy-done.1
  272.7 27.4 %fusion.17 = bf16[8,2,64,2048]{3,2,1,0:T(8,128)(2,1)} fusion(f32[10,2,64,2048]{3,2,1,0:T(8,128)S(1)} %maximum_convert_fusion, f32[2048]{0:T(1024)S(1)} %bitcast.32, f32[2048]{0:T(1024)S(1)} %bitcast.33, f32[2048]{0:T(1024)S(1)} %bitcast.26, f32[2048]{0:T(1024)S(1)} %bitcast.27, f32[2048]{0:T(1024)S(1)} %bitcast.28, f32[2048]{0:T(1024)S(1)} %bitcast.29, ...), kind=kLoop, calls=%fused_computation.25 | loop fusion | flops 174063616 | bytes 39927808 | tf_op jit(solution)/shard_map/convert_element_type | solution.py:59
  300.2 55.7 %all-gather.8.cloned.1.call-done = bf16[2048,4096]{1,0:T(8,128)(2,1)} async-done(((bf16[2048,1024]{1,0:T(8,128)(2,1)}), bf16[2048,4096]{1,0:T(8,128)(2,1)}) %all-gather.8.cloned.1.call-update) | async-done | bytes 16777232 | tf_op jit(solution)/shard_map/all_gather | solution.py:60
  355.9 23.4 %convolution_bitcast_fusion = f32[4096,1024]{0,1:T(8,128)} fusion(bf16[1024,2048]{1,0:T(8,128)(2,1)} %bitcast.22, bf16[2048,4096]{1,0:T(8,128)(2,1)} %all-gather.8.cloned.1.call-done), kind=kOutput, calls=%fused_computation.7 | convolution fusion | flops 17179869184 | bytes 37748736 | tf_op jit(solution)/shard_map/dot_general | solution.py:62
  379.3 0.0 copy-start.2
  379.3 0.0 reduce-scatter.2.cloned.1.call-update
  379.3 280.3 %reduce-scatter.2.cloned.1.call-done = f32[512,1024]{0,1:T(8,128)} async-done(((f32[4096,1024]{0,1:T(8,128)}), f32[512,1024]{0,1:T(8,128)}) %reduce-scatter.2.cloned.1.call-update) | async-done | bytes 2097168 | tf_op jit(solution)/shard_map/reduce_scatter | solution.py:61
  659.6 0.0 copy-done.2
  659.6 2.8 fusion.25
Async XLA Ops:
  6.5 236.2 %copy-start.3 = (f32[2048]{0:T(1024)S(1)}, f32[2048]{0:T(1024)}, u32[]{:S(2)}) copy-start(f32[2048]{0:T(1024)} %param.9) | copy-start | bytes 24580
  6.5 130.5 %all-gather.4.cloned.1.call-start = ((), (), s32[]{:S(2)}) async-start(), calls=%async_computation.1 | async-start | bytes 9437184 | tf_op jit(solution)/shard_map/all_gather | solution.py:50
  7.3 235.5 %all-gather.6.cloned.1.call-start = ((), (), s32[]{:S(2)}) async-start(), calls=%async_computation.2 | async-start | bytes 20971520 | tf_op jit(solution)/shard_map/all_gather | solution.py:48
  8.0 347.9 %all-gather.8.cloned.1.call-start = ((), (), s32[]{:S(2)}) async-start(), calls=%async_computation.3 | async-start | bytes 20971520 | tf_op jit(solution)/shard_map/all_gather | solution.py:60
  8.7 261.2 %copy-start = (f32[9,2048]{1,0:T(8,128)S(1)}, f32[9,2048]{1,0:T(8,128)}, u32[]{:S(2)}) copy-start(f32[9,2048]{1,0:T(8,128)} %param.10) | copy-start | bytes 221188
  8.8 650.8 %reduce-scatter.2.cloned.1.call-start = ((), (), s32[]{:S(2)}) async-start(), calls=%async_computation.4 | async-start | bytes 18874368 | tf_op jit(solution)/shard_map/reduce_scatter | solution.py:61
  265.6 7.2 %copy-start.1 = (f32[2048]{0:T(1024)S(1)}, f32[2048]{0:T(1024)}, u32[]{:S(2)}) copy-start(f32[2048]{0:T(1024)} %param.11) | copy-start | bytes 24580
  265.6 4.4 collective-permute-start.1
  266.9 5.0 collective-permute-start
  379.3 280.3 %copy-start.2 = (f32[512]{0:T(512)S(1)}, f32[512]{0:T(512)}, u32[]{:S(2)}) copy-start(f32[512]{0:T(512)} %param.13) | copy-start | bytes 6148
Sparse Core Ops, SparseCore 0:
  9.4 127.6 all-gather.3
  138.6 104.0 all-gather.5
  244.3 111.5 all-gather.7
  379.4 280.1 reduce-scatter.1
where the time goes:
time: 669 us
  waiting for transfers between devices  574 us (86%)
  matrix products  46.1 us (7%)
  other arithmetic  31.1 us (5%)
  between operations  13.2 us (2%)
    reduce_scatter x1, waiting for transfers between devices, local(): lax.psum_scatter(lax.dot_general(w_cols, act, (((0,), (1,)), ((), ())), p...  280 us
    all_gather x1, waiting for transfers between devices, local(): lax.all_gather(tokens, 'ch', axis=1, tiled=True)  128 us
    all_gather x1, waiting for transfers between devices, local(): w_whole = lax.all_gather(w_in, 'tok', axis=0, tiled=True)  106 us
    all_gather x1, waiting for transfers between devices, local(): w_cols = lax.all_gather(w_out, 'tok', axis=1, tiled=True)  55.7 us
    convert_element_type x1, other arithmetic, local(): jax.nn.gelu(conv, approximate=False).astype(jnp.bfloat16)  27.4 us
    dot_general x1, matrix products, local(): lax.dot_general(w_cols, act, (((0,), (1,)), ((), ())), preferred_element_...  23.4 us
    dot_general x1, matrix products, local(): jnp.dot(lax.all_gather(tokens, 'ch', axis=1, tiled=True), w_whole, prefer...  22.7 us
  transfers between devices with their start and end apart: 6, of which 5 were waited for; matrix products, arithmetic and copies ran while one was open for 8% of the time, Pallas kernels for 0%

commit v1 on v0

--- a/solution.py
+++ b/solution.py
@@ -57,7 +57,12 @@
     padded = pad_columns(fetch_rims(grid).astype(jnp.float32))
     conv = conv_taps(padded, dw_kernel, dw_bias, height, GRIDW)
     act = jax.nn.gelu(conv, approximate=False).astype(jnp.bfloat16).reshape(rows, hidden)
-    w_cols = lax.all_gather(w_out, "tok", axis=1, tiled=True)
+    ring = [w_out]
+    for hop in range(3):
+        ring.append(lax.ppermute(ring[-1], "tok", [(dev, (dev + 1) % 4) for dev in range(4)]))
+    w_cols = jnp.roll(
+        jnp.concatenate(ring[::-1], axis=1), (lax.axis_index("tok") + 1) * ring[0].shape[1], axis=1
+    )
     flipped = lax.psum_scatter(
         lax.dot_general(w_cols, act, (((0,), (1,)), ((), ())), preferred_element_type=jnp.float32),
         "ch",

time: 669 us -> 627 us (0.937)
  waiting for transfers between devices: 574 us -> 498 us
  local copies, waits for them, and re-layouts: 0.17 us -> 33 us
    ppermute x0 -> x3, waiting for transfers between devices: none -> 152 us  [local(): lax.ppermute(ring[-1], 'tok', [(dev, (dev + 1) % 4) for dev in range(4)])]
    all_gather x1, waiting for transfers between devices: 128 us -> 0.01 us  [local(): lax.all_gather(tokens, 'ch', axis=1, tiled=True)]
    all_gather x1 -> x0, waiting for transfers between devices: 55.7 us -> none  [local(): w_cols = lax.all_gather(w_out, 'tok', axis=1, tiled=True)]
    all_gather x1, waiting for transfers between devices: 106 us -> 59.8 us  [local(): w_whole = lax.all_gather(w_in, 'tok', axis=0, tiled=True)]
    unnamed x8 -> x23, local copies, waits for them, and re-layouts: 0.02 us -> 27.9 us
  transfers between devices with their start and end apart: 6 -> 8, of which waited for: 5 -> 5; matrix products, arithmetic and copies ran while one was open for 8% -> 5% of each run, Pallas kernels for 0% -> 0%
where the time goes in v1:
time: 627 us
  waiting for transfers between devices  498 us (79%)
  matrix products  46.4 us (7%)
  local copies, waits for them, and re-layouts  33 us (5%)
  other arithmetic  30 us (5%)
  between operations  13.2 us (2%)
    reduce_scatter x1, waiting for transfers between devices, local(): lax.psum_scatter(lax.dot_general(w_cols, act, (((0,), (1,)), ((), ())), p...  285 us
    ppermute x3, waiting for transfers between devices, local(): lax.ppermute(ring[-1], 'tok', [(dev, (dev + 1) % 4) for dev in range(4)])  152 us
    all_gather x1, waiting for transfers between devices, local(): w_whole = lax.all_gather(w_in, 'tok', axis=0, tiled=True)  59.8 us
    unnamed x23, local copies, waits for them, and re-layouts  27.9 us
    convert_element_type x1, other arithmetic, local(): jax.nn.gelu(conv, approximate=False).astype(jnp.bfloat16)  27.4 us
    dot_general x1, matrix products, local(): lax.dot_general(w_cols, act, (((0,), (1,)), ((), ())), preferred_element_...  23.6 us
    dot_general x1, matrix products, local(): jnp.dot(lax.all_gather(tokens, 'ch', axis=1, tiled=True), w_whole, prefer...  22.8 us
  transfers between devices with their start and end apart: 8, of which 5 were waited for; matrix products, arithmetic and copies ran while one was open for 5% of the time, Pallas kernels for 0%

profile of v1, /device:TPU:0, one launch (start us, length us, event | category | flops | bytes accessed | tf_op | source)
XLA Modules:
  0.0 626.6 jit_solution(5711182243731829285)
XLA Ops:
  6.5 0.0 all-gather.3.cloned.1.call-start
  6.5 0.7 all-gather.3.cloned.1.call-update
  7.3 0.0 all-gather.5.cloned.1.call-start
  7.3 0.7 all-gather.5.cloned.1.call-update
  8.0 0.0 reduce-scatter.2.cloned.1.call-start
  8.1 0.5 collective-permute-start
  8.6 48.3 %collective-permute-done = bf16[2048,1024]{1,0:T(8,128)(2,1)S(1)} collective-permute-done((bf16[2048,1024]{1,0:T(8,128)(2,1)}, bf16[2048,1024]{1,0:T(8,128)(2,1)S(1)}, u32[]{:S(2)}, u32[]{:S(2)}) %collective-permute-start) | collective-permute-done | bytes 4194336 | tf_op jit(solution)/shard_map/ppermute | solution.py:62
  56.9 0.0 copy-start.2
  56.9 1.9 copy-done.2
  58.9 0.0 collective-permute-start.1
  58.9 48.0 %collective-permute-done.1 = bf16[2048,1024]{1,0:T(8,128)(2,1)} collective-permute-done((bf16[2048,1024]{1,0:T(8,128)(2,1)S(1)}, bf16[2048,1024]{1,0:T(8,128)(2,1)}, u32[]{:S(2)}, u32[]{:S(2)}) %collective-permute-start.1) | collective-permute-done | bytes 4194336 | tf_op jit(solution)/shard_map/ppermute | solution.py:62
  106.9 0.0 collective-permute-start.2
  106.9 1.3 fusion.30
  108.2 0.0 copy-start.3
  108.2 55.5 %collective-permute-done.2 = bf16[2048,1024]{1,0:T(8,128)(2,1)} collective-permute-done((bf16[2048,1024]{1,0:T(8,128)(2,1)}, bf16[2048,1024]{1,0:T(8,128)(2,1)}, u32[]{:S(2)}, u32[]{:S(2)}) %collective-permute-start.2) | collective-permute-done | bytes 4194336 | tf_op jit(solution)/shard_map/ppermute | solution.py:62
  163.7 4.6 constant_dynamic-update-slice_fusion.7
  168.3 0.0 copy-start
  168.3 4.8 constant_dynamic-update-slice_fusion.6
  173.1 0.0 copy-done.3
  173.1 2.4 constant_dynamic-update-slice_fusion.5
  175.5 0.0 copy-done
  175.5 2.5 constant_dynamic-update-slice_fusion.4
  178.0 0.0 copy-start.7
  178.0 4.7 constant_dynamic-update-slice_fusion.3
  182.7 4.6 constant_dynamic-update-slice_fusion.2
  187.3 0.0 all-gather.3.cloned.1.call-done
  187.3 59.8 %all-gather.5.cloned.1.call-done = bf16[4096,2048]{1,0:T(8,128)(2,1)} async-done(((bf16[1024,2048]{1,0:T(8,128)(2,1)}), bf16[4096,2048]{1,0:T(8,128)(2,1)}) %all-gather.5.cloned.1.call-update) | async-done | bytes 16777232 | tf_op jit(solution)/shard_map/all_gather | solution.py:48
  247.1 0.0 copy-done.7
  247.1 22.8 %add_convert_fusion = bf16[1024,2048]{1,0:T(8,128)(2,1)S(1)} fusion(bf16[1024,4096]{1,0:T(8,128)(2,1)} %all-gather.3.cloned.1.call-done, bf16[4096,2048]{1,0:T(8,128)(2,1)} %all-gather.5.cloned.1.call-done, f32[2048]{0:T(1024)S(1)} %copy-done.7), kind=kOutput, calls=%fused_computation.43 | convolution fusion | flops 17184063488 | bytes 29368320 | tf_op jit(solution)/shard_map/dot_general | solution.py:49
  269.9 0.0 copy-start.1
  269.9 0.1 fusion.29
  270.0 1.6 collective-permute-start.4
  271.6 3.2 collective-permute-start.3
  274.8 0.0 copy-done.4
  274.9 2.4 constant_dynamic-update-slice_fusion.1
  277.3 0.0 copy-done.1
  277.3 2.4 constant_dynamic-update-slice_fusion
  279.6 0.0 collective-permute-done.4
  279.6 0.0 collective-permute-done.3
  279.7 0.8 maximum_convert_fusion
  280.5 0.0 copy-done.5
  280.5 27.4 %fusion.19 = bf16[8,2,64,2048]{3,2,1,0:T(8,128)(2,1)} fusion(f32[10,2,64,2048]{3,2,1,0:T(8,128)S(1)} %maximum_convert_fusion, f32[2048]{0:T(1024)S(1)} %bitcast.29, f32[2048]{0:T(1024)S(1)} %bitcast.30, f32[2048]{0:T(1024)S(1)} %bitcast.23, f32[2048]{0:T(1024)S(1)} %bitcast.24, f32[2048]{0:T(1024)S(1)} %bitcast.25, f32[2048]{0:T(1024)S(1)} %bitcast.26, ...), kind=kLoop, calls=%fused_computation.26 | loop fusion | flops 174063616 | bytes 39927808 | tf_op jit(solution)/shard_map/convert_element_type | solution.py:59
  307.9 23.6 %fusion = f32[4096,1024]{1,0:T(8,128)} fusion(bf16[1024,2048]{1,0:T(8,128)(2,1)} %bitcast.19, bf16[2048,8192]{1,0:T(8,128)(2,1)} %constant_dynamic-update-slice_fusion, s32[]{:T(128)S(6)} %select_n.14), kind=kOutput, calls=%fused_computation | convolution fusion | flops 17179869184 | bytes 37748740 | tf_op jit(solution)/shard_map/dot_general | solution.py:67
  331.6 0.0 reduce-scatter.2.cloned.1.call-update
  331.6 285.4 %reduce-scatter.2.cloned.1.call-done = f32[512,1024]{1,0:T(8,128)} async-done(((f32[4096,1024]{1,0:T(8,128)}), f32[512,1024]{1,0:T(8,128)}) %reduce-scatter.2.cloned.1.call-update) | async-done | bytes 2097168 | tf_op jit(solution)/shard_map/reduce_scatter | solution.py:66
  617.0 0.0 copy-done.6
  617.0 1.8 fusion.27
  618.8 1.3 copy.8
  (3 shorter events, 0.0 us)
Async XLA Ops:
  6.5 180.8 %all-gather.3.cloned.1.call-start = ((), (), s32[]{:S(2)}) async-start(), calls=%async_computation.1 | async-start | bytes 9437184 | tf_op jit(solution)/shard_map/all_gather | solution.py:50
  7.3 239.8 %all-gather.5.cloned.1.call-start = ((), (), s32[]{:S(2)}) async-start(), calls=%async_computation.2 | async-start | bytes 20971520 | tf_op jit(solution)/shard_map/all_gather | solution.py:48
  8.0 609.0 %reduce-scatter.2.cloned.1.call-start = ((), (), s32[]{:S(2)}) async-start(), calls=%async_computation.3 | async-start | bytes 18874368 | tf_op jit(solution)/shard_map/reduce_scatter | solution.py:66
  8.1 48.9 %collective-permute-start = (bf16[2048,1024]{1,0:T(8,128)(2,1)}, bf16[2048,1024]{1,0:T(8,128)(2,1)S(1)}, u32[]{:S(2)}, u32[]{:S(2)}) collective-permute-start(bf16[2048,1024]{1,0:T(8,128)(2,1)} %param.12), channel_id=1, source_target_pairs={{0,8},{8,16},{16,24},{24,0},{1,9},{9,17},{17,25},{25,1},{2,10},{10... | collective-permute-start | bytes 12582920 | tf_op jit(solution)/shard_map/ppermute | solution.py:62
  56.9 1.9 copy-start.2
  58.9 48.0 %collective-permute-start.1 = (bf16[2048,1024]{1,0:T(8,128)(2,1)S(1)}, bf16[2048,1024]{1,0:T(8,128)(2,1)}, u32[]{:S(2)}, u32[]{:S(2)}) collective-permute-start(bf16[2048,1024]{1,0:T(8,128)(2,1)S(1)} %collective-permute-done), channel_id=1, source_target_pairs={{0,8},{8,16},{16,24},{24,0},{1,9},{9,17},{17,25},{25,1},{2,10},{10... | collective-permute-start | bytes 12582920 | tf_op jit(solution)/shard_map/ppermute | solution.py:62
  106.9 56.8 %collective-permute-start.2 = (bf16[2048,1024]{1,0:T(8,128)(2,1)}, bf16[2048,1024]{1,0:T(8,128)(2,1)}, u32[]{:S(2)}, u32[]{:S(2)}) collective-permute-start(bf16[2048,1024]{1,0:T(8,128)(2,1)} %collective-permute-done.1), channel_id=1, source_target_pairs={{0,8},{8,16},{16,24},{24,0},{1,9},{9,17},{17,25},{25,1},{2,10},{10... | collective-permute-start | bytes 12582920 | tf_op jit(solution)/shard_map/ppermute | solution.py:62
  108.2 64.8 %copy-start.3 = (bf16[2048,1024]{1,0:T(8,128)(2,1)S(1)}, bf16[2048,1024]{1,0:T(8,128)(2,1)}, u32[]{:S(2)}) copy-start(bf16[2048,1024]{1,0:T(8,128)(2,1)} %copy-done.2) | copy-start | bytes 12582916
  168.3 7.2 %copy-start = (bf16[2048,1024]{1,0:T(8,128)(2,1)S(1)}, bf16[2048,1024]{1,0:T(8,128)(2,1)}, u32[]{:S(2)}) copy-start(bf16[2048,1024]{1,0:T(8,128)(2,1)} %param.12) | copy-start | bytes 12582916
  178.0 69.1 %copy-start.7 = (f32[2048]{0:T(1024)S(1)}, f32[2048]{0:T(1024)}, u32[]{:S(2)}) copy-start(f32[2048]{0:T(1024)} %param.9) | copy-start | bytes 24580
  247.1 27.8 %copy-start.4 = (bf16[2048,1024]{1,0:T(8,128)(2,1)S(1)}, bf16[2048,1024]{1,0:T(8,128)(2,1)}, u32[]{:S(2)}) copy-start(bf16[2048,1024]{1,0:T(8,128)(2,1)} %copy-done.2) | copy-start | bytes 12582916
  269.9 7.4 %copy-start.1 = (bf16[2048,1024]{1,0:T(8,128)(2,1)S(1)}, bf16[2048,1024]{1,0:T(8,128)(2,1)}, u32[]{:S(2)}) copy-start(bf16[2048,1024]{1,0:T(8,128)(2,1)} %param.12) | copy-start | bytes 12582916
  270.0 9.6 %collective-permute-start.4 = (bf16[1,2,64,2048]{3,2,1,0:T(8,128)(2,1)S(1)}, bf16[1,2,64,2048]{3,2,1,0:T(8,128)(2,1)S(1)}, u32[]{:S(2)}, u32[]{:S(2)}) collective-permute-start(bf16[1,2,64,2048]{3,2,1,0:T(8,128)(2,1)S(1)} %bitcast.21), channel_id=1, source_target_pairs={{8,0},{16,8},{24,16},{9,1},{17,9},{25,17},{10,2},{18,10},{26,18},{... | collective-permute-start | bytes 1572872 | tf_op jit(solution)/shard_map/ppermute | solution.py:18
  271.6 8.1 %collective-permute-start.3 = (bf16[1,2,64,2048]{3,2,1,0:T(8,128)(2,1)S(1)}, bf16[1,2,64,2048]{3,2,1,0:T(8,128)(2,1)S(1)}, u32[]{:S(2)}, u32[]{:S(2)}) collective-permute-start(bf16[1,2,64,2048]{3,2,1,0:T(8,128)(2,1)S(1)} %bitcast.20), channel_id=1, source_target_pairs={{0,8},{8,16},{16,24},{1,9},{9,17},{17,25},{2,10},{10,18},{18,26},{... | collective-permute-start | bytes 1572872 | tf_op jit(solution)/shard_map/ppermute | solution.py:17
  279.6 0.9 copy-start.5
  331.6 285.4 %copy-start.6 = (f32[512]{0:T(512)S(1)}, f32[512]{0:T(512)}, u32[]{:S(2)}) copy-start(f32[512]{0:T(512)} %param.13) | copy-start | bytes 6148
Sparse Core Ops, SparseCore 0:
  9.4 127.6 all-gather.2
  138.6 108.4 all-gather.4
  331.7 285.2 reduce-scatter.1
